TPU v7x, 32 devices: a whole 2x2x4 slice. The times are simulated.
32 devices in a mesh: groups: 2 (over x), seq: 16 (over z, y, core).
Axes of the slice: x: 2, y: 2, z: 4, core: 2. Of those that a mesh axis runs over, the one named last changes fastest.
Arguments:
- query: bfloat16 [2048, 4096], P(('groups', 'seq')), parts along dimension 0, may hold values from -28 to 28
- keys: bfloat16 [2048, 512], P(('groups', 'seq')), parts along dimension 0, may hold values from -4 to 4
- values: bfloat16 [2048, 512], P(('groups', 'seq')), parts along dimension 0, may hold values from -6 to 6
- query_bias: bfloat16 [4096], P('seq'), may hold values from -3 to 3
- key_bias: bfloat16 [512], P('seq'), may hold values from -3 to 3
- value_projection_bias: bfloat16 [512], P('seq'), may hold values from -3 to 3
- frame_order: int32 [128], P(('groups', 'seq')), parts along dimension 0, may hold values from 0 to 63, each once
Outputs:
- attended: bfloat16 [2048, 4096], P(('groups', 'seq')), parts along dimension 0
There are 2 independent parts, one for each index of `groups`. A program takes and returns all parts, laid end to end along the dimension named above; an argument that names none is the same for every part. Nothing has to cross between parts.
Inputs may be any that keep to these rules, and one draw needn't show every extreme that they name: `frame_order`: each of the 64 frames stands in exactly one slot.
All inputs are finite; a program needn't handle non-finite values.
Results may differ from a plain program's by a relative error of at most 0.011.
Values may be sent and summed in bfloat16 or wider, within the bound.
A program may use at most 64 MiB of HBM per device.

v0:
```python
import functools
import math

import jax
import jax.numpy as jnp
import numpy as np
from jax import lax
from jax.experimental import pallas as pl
from jax.experimental.pallas import tpu as pltpu
from jax.sharding import PartitionSpec as P

HEAD = 128
HALF = HEAD // 2
QH = 32
KVH = 4
RATIO = QH // KVH
GRID = 4
FRAME_TOK = 16
MESH = pl.DeviceIdType.MESH
NEG = -1e30
PIECES = 2
PAIRS_T = HALF // 4
PAIRS_R = HALF // 4 + 3 * HALF // 8


def tables():
    pair = np.arange(HEAD) % HALF
    freq = np.exp(-(2.0 * pair / HEAD) * math.log(1000000.0))
    tok = np.arange(FRAME_TOK)
    source = np.where(pair[None, :] < PAIRS_R, (tok // GRID)[:, None], (tok % GRID)[:, None])
    angle = source * freq[None, :]
    sign = np.where(np.arange(HEAD) < HALF, -1.0, 1.0)
    rows = np.zeros((40, HEAD), np.float32)
    rows[0:16] = np.cos(angle)
    rows[16:32] = np.sin(angle) * sign[None, :]
    rows[32] = 2.0 * freq
    return rows


def cos_sin(frames, spatial):
    angle = frames * spatial[32:33, :]
    turns = jnp.round(angle * (1.0 / (2.0 * math.pi)))
    angle = angle - turns * 6.28125
    angle = angle - turns * (2.0 * math.pi - 6.28125)
    lane = lax.broadcasted_iota(jnp.int32, (FRAME_TOK, HEAD), 1)
    temporal = lane % HALF < PAIRS_T
    sign = jnp.where(lane < HALF, -1.0, 1.0)
    cos_t, sin_t = jnp.cos(angle), jnp.sin(angle)
    cosines, sines = [], []
    for j in range(frames.shape[0]):
        cosines.append(jnp.where(temporal, cos_t[j : j + 1, :], spatial[0:16, :]))
        sines.append(jnp.where(temporal, sin_t[j : j + 1, :] * sign, spatial[16:32, :]))
    return jnp.concatenate(cosines, axis=0), jnp.concatenate(sines, axis=0)


def spin(x, cosine, sine):
    return x * cosine + pltpu.roll(x, HALF, 1) * sine


def kernel(
    A, B, n, qper,
    q_hbm, k_hbm, v_hbm, qb_hbm, kb_hbm, vb_hbm, order_hbm, tab_hbm,
    o_ref,
    qb_ref, kb_ref, vb_ref, order_ref, tab_ref,
    q_ref, pack_ref, kbuf, vbuf, pbuf, qs, acc, top, den, ksc, vsc, hide,
    recv, send, precv, psend, load,
):
    me = lax.axis_index("seq")
    rows = kbuf.shape[1]
    frames = rows // FRAME_TOK
    cut = rows // (PIECES // 2)
    core = me % 2
    b = (me // 2) % B
    a = me // (2 * B)

    def piece(p, s):
        return (kbuf, vbuf)[p % 2].at[s, pl.ds((p // 2) * cut, cut)]

    def slot(x, y, z):
        return (x * B + y) * 2 + z

    ways = (
        (a + 1 < A, slot(a + 1, b, core)),
        (a > 0, slot(a - 1, b, core)),
        (b + 1 < B, slot(a, b + 1, core)),
        (b > 0, slot(a, b - 1, core)),
        (None, slot(a, b, 1 - core)),
    )

    def copy(t, s, way):
        return pltpu.make_async_remote_copy(
            src_ref=piece(t, s),
            dst_ref=piece(t, s),
            send_sem=send.at[t, way, s],
            recv_sem=recv.at[t, s],
            device_id={"seq": ways[way][1]},
            device_id_type=MESH,
        )

    def when(cond, act):
        if cond is None:
            act()
        else:
            pl.when(cond)(act)

    def fan(t, s, dirs, start):
        for way in dirs:
            c = copy(t, s, way)
            when(ways[way][0], c.start if start else c.wait_send)

    def arrive(t, s):
        copy(t, s, 4).wait_recv()

    def inside(i, size):
        return jnp.logical_and(i >= 0, i < size)

    def along_a(d, start):
        for t in range(PIECES):
            for sg in (1, -1):
                x = a + sg * d

                @pl.when(jnp.logical_and(inside(x, A), d < A))
                def _(x=x, sg=sg, t=t):
                    s = slot(x, b, core)
                    if start:
                        arrive(t, s)
                    fan(t, s, (1 if sg > 0 else 0, 2, 3, 4), start)

    def along_b(d, start):
        for e in range(1, B):
            for t in range(PIECES):
                for sg in (1, -1):
                    x = a + sg * d
                    ok = inside(x, A) if sg > 0 else jnp.logical_and(inside(x, A), d > 0)
                    for sb in (1, -1):
                        y = b + sb * e

                        @pl.when(jnp.logical_and(ok, inside(y, B)))
                        def _(x=x, y=y, sb=sb, t=t):
                            s = slot(x, y, core)
                            if start:
                                arrive(t, s)
                            fan(t, s, (3 if sb > 0 else 2, 4), start)

    barrier = pltpu.get_barrier_semaphore()

    def greet(i, _):
        pl.semaphore_signal(barrier, inc=1, device_id={"seq": lax.rem(me + i, n)}, device_id_type=MESH)
        return 0

    lax.fori_loop(1, n, greet, 0)
    k_load = pltpu.make_async_copy(k_hbm, kbuf.at[me], load.at[0])
    v_load = pltpu.make_async_copy(v_hbm, vbuf.at[me], load.at[1])
    q_load = pltpu.make_async_copy(q_hbm, q_ref, load.at[2])
    small = [
        pltpu.make_async_copy(src, dst, load.at[3 + i])
        for i, (src, dst) in enumerate((
            (order_hbm, order_ref), (qb_hbm, qb_ref), (kb_hbm, kb_ref), (vb_hbm, vb_ref), (tab_hbm, tab_ref),
        ))
    ]
    for c in small + [k_load, v_load, q_load]:
        c.start()

    lane = lax.broadcasted_iota(jnp.int32, (1, HEAD), 1)

    def placed(values):
        size = values.shape[1]
        spots = HEAD // size
        return jnp.where(lane // size == me % spots, jnp.concatenate([values] * spots, axis=1), 0.0)

    def row(ref):
        return ref[...].astype(jnp.float32)[None, :]

    for c in small:
        c.wait()
    pack_ref[...] = jnp.zeros_like(pack_ref)
    q_row = row(qb_ref)
    if qper >= HEAD:
        for i in range(qper // HEAD):
            pack_ref[i : i + 1, :] = q_row[:, i * HEAD : (i + 1) * HEAD]
    else:
        pack_ref[0:1, :] = placed(q_row)
    pack_ref[2:3, :] = placed(row(kb_ref))
    pack_ref[3:4, :] = placed(row(vb_ref))
    qpos = (lane % FRAME_TOK).astype(jnp.float32)
    for f in range(frames):
        frame = order_ref[f].astype(jnp.float32)
        pack_ref[8 - frames + f : 9 - frames + f, :] = jnp.full((1, HEAD), 1.0, jnp.float32) * frame
        qpos = qpos + jnp.where((lane % rows) // FRAME_TOK == f, frame * FRAME_TOK, 0.0)
    pbuf[me] = pack_ref[...]
    tab = tab_ref[...]
    q_cos, q_sin = cos_sin(pack_ref[8 - frames :, :], tab)
    fold = math.log2(math.e) / math.sqrt(HEAD)
    q_cos, q_sin = q_cos * fold, q_sin * fold
    k_load.wait()
    v_load.wait()
    pl.semaphore_wait(barrier, n - 1)

    def pack_copy(i, s):
        return pltpu.make_async_remote_copy(
            src_ref=pack_ref,
            dst_ref=pbuf.at[s],
            send_sem=psend.at[i],
            recv_sem=precv.at[s],
            device_id={"seq": lax.rem(me + i, n)},
            device_id_type=MESH,
        )

    def push(i, _):
        pack_copy(i, me).start()
        return 0

    lax.fori_loop(1, n, push, 0)
    for t in range(PIECES):
        fan(t, me, (0, 1, 2, 3, 4), True)

    acc[...] = jnp.zeros_like(acc)
    den[...] = jnp.zeros_like(den)
    top[...] = jnp.full_like(top, NEG)

    def pulled(i, _):
        pack_copy(i, lax.rem(me + i, n)).wait_recv()
        return 0

    lax.fori_loop(1, n, pulled, 0)
    q_load.wait()

    for h in range(QH):
        if qper >= HEAD:
            per = qper // HEAD
            bias = pbuf[h // per, h % per : h % per + 1, :]
        else:
            parts = HEAD // qper
            bias = sum(pbuf[h * parts + i, 0:1, :] for i in range(parts))
        x = q_ref[:, h * HEAD : (h + 1) * HEAD].astype(jnp.float32) + bias
        at = (h % RATIO) * rows
        qs[h // RATIO, at : at + rows, :] = spin(x, q_cos, q_sin).astype(jnp.bfloat16)
    share = n // KVH
    k_bias = [sum(pbuf[g * share + i, 2:3, :] for i in range(share)) for g in range(KVH)]
    v_bias = [sum(pbuf[g * share + i, 3:4, :] for i in range(share)) for g in range(KVH)]
    within = lax.broadcasted_iota(jnp.int32, (FRAME_TOK, HEAD), 0).astype(jnp.float32)

    def chunk(first):
        for j in range(4):
            s = first + j
            order = pbuf[s][8 - frames :, :]
            cosine, sine = cos_sin(order, tab)
            for f in range(frames):
                kpos = order[f : f + 1, :] * FRAME_TOK + within
                at = j * rows + f * FRAME_TOK
                hide[at : at + FRAME_TOK, :] = jnp.where(kpos <= qpos, 0.0, NEG)
            for g in range(KVH):
                cols = slice(g * HEAD, (g + 1) * HEAD)
                x = kbuf[s, :, cols].astype(jnp.float32) + k_bias[g]
                ksc[g, j * rows : (j + 1) * rows, :] = spin(x, cosine, sine).astype(jnp.bfloat16)
                y = vbuf[s, :, cols].astype(jnp.float32) + v_bias[g]
                vsc[g, j * rows : (j + 1) * rows, :] = y.astype(jnp.bfloat16)
        for g in range(KVH):
            scores = lax.dot_general(
                ksc[g], qs[g], (((1,), (1,)), ((), ())), preferred_element_type=jnp.float32
            )
            mask = hide[...]
            scores = scores + jnp.concatenate([mask] * (scores.shape[1] // HEAD), axis=1)
            old = top[g]
            new = jnp.maximum(old, jnp.max(scores, axis=0, keepdims=True))
            expo = jnp.exp2(scores - new)
            factor = jnp.exp2(old - new)
            top[g] = new
            den[g] = den[g] * factor + jnp.sum(expo, axis=0, keepdims=True)
            acc[g] = acc[g] * factor + lax.dot_general(
                vsc[g], expo.astype(jnp.bfloat16), (((0,), (0,)), ((), ())),
                preferred_element_type=jnp.float32,
            )

    low = a < A // 2
    mirror = jnp.where(low, a, A - 1 - a)

    def step(d, _):
        along_a(d + 1, True)
        along_b(d, True)
        near = jnp.where(d % 2 == 1, -((d + 1) // 2), d // 2)
        plane = mirror + jnp.where(d <= 2 * mirror, near, d - mirror)
        plane = jnp.where(low, plane, A - 1 - plane)
        for y in range(B):
            for t in range(PIECES):
                arrive(t, slot(plane, y, 1 - core))
        if 2 * B == 4:
            chunk(plane * 4)
        else:
            def part(i, _):
                chunk(plane * 2 * B + i * 4)
                return 0

            lax.fori_loop(0, 2 * B // 4, part, 0)
        return 0

    lax.fori_loop(0, A, step, 0)

    for g in range(KVH):
        mixed = acc[g] * (1.0 / den[g])
        flat = mixed.T.astype(jnp.bfloat16)
        for r in range(RATIO):
            h = g * RATIO + r
            o_ref[:, h * HEAD : (h + 1) * HEAD] = flat[r * rows : (r + 1) * rows, :]

    for t in range(PIECES):
        fan(t, me, (0, 1, 2, 3, 4), False)

    def drain(d, _):
        along_a(d + 1, False)
        along_b(d, False)
        return 0

    lax.fori_loop(0, A, drain, 0)

    def pushed(i, _):
        pack_copy(i, me).wait_send()
        return 0

    lax.fori_loop(1, n, pushed, 0)


def on_device(n, query, keys, values, query_bias, key_bias, value_projection_bias, frame_order):
    chips = n // 2
    B = 1
    while B * B * 4 <= chips:
        B *= 2
    A = chips // B
    rows = keys.shape[0]
    qper = query_bias.shape[0]
    wide = RATIO * rows
    keys_at_once = 4 * rows
    whole = pl.BlockSpec(memory_space=pltpu.VMEM)
    far = pl.BlockSpec(memory_space=pltpu.HBM)
    return pl.pallas_call(
        functools.partial(kernel, A, B, n, qper),
        out_shape=jax.ShapeDtypeStruct(query.shape, jnp.bfloat16),
        in_specs=[far] * 8,
        out_specs=whole,
        scratch_shapes=[
            pltpu.VMEM(query_bias.shape, jnp.bfloat16),
            pltpu.VMEM(key_bias.shape, jnp.bfloat16),
            pltpu.VMEM(key_bias.shape, jnp.bfloat16),
            pltpu.SMEM(frame_order.shape, jnp.int32),
            pltpu.VMEM((40, HEAD), jnp.float32),
            pltpu.VMEM(query.shape, jnp.bfloat16),
            pltpu.VMEM((8, HEAD), jnp.float32),
            pltpu.VMEM((n, rows, KVH * HEAD), jnp.bfloat16),
            pltpu.VMEM((n, rows, KVH * HEAD), jnp.bfloat16),
            pltpu.VMEM((n, 8, HEAD), jnp.float32),
            pltpu.VMEM((KVH, wide, HEAD), jnp.bfloat16),
            pltpu.VMEM((KVH, HEAD, wide), jnp.float32),
            pltpu.VMEM((KVH, 1, wide), jnp.float32),
            pltpu.VMEM((KVH, 1, wide), jnp.float32),
            pltpu.VMEM((KVH, keys_at_once, HEAD), jnp.bfloat16),
            pltpu.VMEM((KVH, keys_at_once, HEAD), jnp.bfloat16),
            pltpu.VMEM((keys_at_once, HEAD), jnp.float32),
            pltpu.SemaphoreType.DMA((PIECES, n)),
            pltpu.SemaphoreType.DMA((PIECES, 5, n)),
            pltpu.SemaphoreType.DMA((n,)),
            pltpu.SemaphoreType.DMA((n,)),
            pltpu.SemaphoreType.DMA((8,)),
        ],
        compiler_params=pltpu.CompilerParams(vmem_limit_bytes=(16 if n <= 32 else 48) << 20, collective_id=0, has_side_effects=True),
    )(*(
        pltpu.with_memory_space_constraint(x, pltpu.HBM)
        for x in (
            query, keys, values, query_bias, key_bias, value_projection_bias, frame_order,
            jnp.asarray(tables()),
        )
    ))


def solution(mesh):
    placed = (
        P(("groups", "seq"), None),
        P(("groups", "seq"), None),
        P(("groups", "seq"), None),
        P("seq"),
        P("seq"),
        P("seq"),
        P(("groups", "seq")),
    )
    return jax.shard_map(
        functools.partial(on_device, mesh.shape["seq"]),
        mesh=mesh,
        in_specs=placed,
        out_specs=P(("groups", "seq"), None),
        check_vma=False,
    )
```

profile of v0, /device:TPU:1, one launch (start us, length us, event | category | flops | bytes accessed | tf_op | source)
XLA Modules:
  0.0 28.5 jit_solution(17972527970564664318)
XLA Ops:
  0.0 27.7 %shard_map.82 = bf16[64,4096]{1,0:T(8,128)(2,1)S(1)} custom-call(bf16[64,4096]{1,0:T(8,128)(2,1)} %q_hbm.1, bf16[64,512]{1,0:T(8,128)(2,1)} %k_hbm.1, bf16[64,512]{1,0:T(8,128)(2,1)} %v_hbm.1, bf16[256]{0:T(256)(128)(2,1)} %qb_hbm.1, bf16[32]{0:T(256)(128)(2,1)} %kb_hbm.1, bf16[32]{0:T(256)(128)(2,1)} %vb_hbm.1, s32[4]{0:T(128)} %order_hbm.1, ...), custom_call_target="tpu_custom_call" | custom-call | tf_op jit(solution)/shard_map/pallas_call | solution.py:335
  27.7 0.8 %copy.10 = bf16[64,4096]{1,0:T(8,128)(2,1)} copy(bf16[64,4096]{1,0:T(8,128)(2,1)S(1)} %shard_map.82) | data formatting | bytes 1048576
where the time goes:
time: 28.6 us; the launch traced here: 28.5 us
  Pallas kernels  27.7 us (97%)
  local copies, waits for them, and re-layouts  0.8 us (3%)
    pallas_call x1, Pallas kernels, on_device(): pl.pallas_call(functools.partial(kernel, A, B, n, qper), out_shape=jax.Sh...  27.7 us
    unnamed x1, local copies, waits for them, and re-layouts  0.8 us

commit v1 on v0

--- a/solution.py
+++ b/solution.py
@@ -320,6 +320,372 @@
     lax.fori_loop(1, n, pushed, 0)
 
 
+UP, DOWN, ACROSS, SIDE = range(4)
+
+
+def near_kernel(
+    A, n, qper,
+    q_hbm, k_hbm, v_hbm, qb_hbm, kb_hbm, vb_hbm, order_hbm, tab_hbm,
+    o_ref,
+    qb_ref, kb_ref, vb_ref, order_ref, tab_ref,
+    q_ref, kbuf, vbuf, pbuf, cosb, sinb, qs, acc, top, den, fac, ksc, vsc, prob, hide,
+    recv, send, precv, psend, zrecv, zsend, load, token,
+):
+    me = lax.axis_index("seq")
+    rows = kbuf.shape[1]
+    frames = rows // FRAME_TOK
+    plane_size = 4
+    core = me % 2
+    b = (me // 2) % 2
+    a = me // plane_size
+
+    def slot(x, y, z):
+        return (x * 2 + y) * 2 + z
+
+    ways = (
+        (a + 1 < A, slot(a + 1, b, core)),
+        (a > 0, slot(a - 1, b, core)),
+        (None, slot(a, 1 - b, core)),
+        (None, slot(a, b, 1 - core)),
+    )
+    mates = (slot(a, b, 1 - core), slot(a, 1 - b, core), slot(a, 1 - b, 1 - core))
+
+    def when(cond, act):
+        if cond is None:
+            act()
+        else:
+            pl.when(cond)(act)
+
+    def both(one, two):
+        return two if one is None else jnp.logical_and(one, two)
+
+    def copy(t, s, way):
+        piece = (kbuf, vbuf)[t].at[s]
+        return pltpu.make_async_remote_copy(
+            src_ref=piece, dst_ref=piece,
+            send_sem=send.at[t, way, s], recv_sem=recv.at[t, s],
+            device_id={"seq": ways[way][1]}, device_id_type=MESH,
+        )
+
+    def go(t, s, way):
+        when(ways[way][0], copy(t, s, way).start)
+
+    def arrive(t, s):
+        copy(t, s, SIDE).wait_recv()
+
+    def mate_copy(i, s):
+        return pltpu.make_async_remote_copy(
+            src_ref=pbuf.at[s], dst_ref=pbuf.at[s],
+            send_sem=psend.at[i], recv_sem=precv.at[i],
+            device_id={"seq": mates[i]}, device_id_type=MESH,
+        )
+
+    def far_copy(x, p):
+        rows_of = pbuf.at[pl.ds(p * plane_size, plane_size)]
+        return pltpu.make_async_remote_copy(
+            src_ref=rows_of, dst_ref=rows_of,
+            send_sem=zsend.at[x], recv_sem=zrecv.at[p],
+            device_id={"seq": slot(x, b, core)}, device_id_type=MESH,
+        )
+
+    def inside(x):
+        return jnp.logical_and(x >= 0, x < A)
+
+    barrier = pltpu.get_barrier_semaphore()
+
+    def greet(s):
+        pl.semaphore_signal(barrier, inc=1, device_id={"seq": s}, device_id_type=MESH)
+
+    for s in mates:
+        greet(s)
+    for way in (UP, DOWN):
+        when(ways[way][0], functools.partial(greet, ways[way][1]))
+
+    small = [
+        pltpu.make_async_copy(src, dst, load.at[3 + i])
+        for i, (src, dst) in enumerate((
+            (order_hbm, order_ref), (qb_hbm, qb_ref), (kb_hbm, kb_ref), (vb_hbm, vb_ref), (tab_hbm, tab_ref),
+        ))
+    ]
+    k_load = pltpu.make_async_copy(k_hbm, kbuf.at[me], load.at[0])
+    v_load = pltpu.make_async_copy(v_hbm, vbuf.at[me], load.at[1])
+    q_load = pltpu.make_async_copy(q_hbm, q_ref, load.at[2])
+    for c in small + [k_load, v_load, q_load]:
+        c.start()
+
+    lane = lax.broadcasted_iota(jnp.int32, (1, HEAD), 1)
+
+    def placed(values):
+        spots = HEAD // values.shape[1]
+        return jnp.where(lane // values.shape[1] == me % spots, jnp.concatenate([values] * spots, axis=1), 0.0)
+
+    def row(ref):
+        return ref[...].astype(jnp.float32)[None, :]
+
+    for c in small:
+        c.wait()
+    per = qper // HEAD
+    q_row = row(qb_ref)
+    parts = [q_row[:, i * HEAD : (i + 1) * HEAD] for i in range(per)]
+    parts += [jnp.zeros((1, HEAD), jnp.float32)] * (2 - per)
+    parts += [placed(row(kb_ref)), placed(row(vb_ref))]
+    qpos = (lane % FRAME_TOK).astype(jnp.float32)
+    for f in range(frames):
+        frame = order_ref[f].astype(jnp.float32)
+        parts.append(jnp.full((1, HEAD), 1.0, jnp.float32) * frame)
+        qpos = qpos + jnp.where((lane % rows) // FRAME_TOK == f, frame * FRAME_TOK, 0.0)
+    pbuf[me] = jnp.concatenate(parts, axis=0)
+    k_load.wait()
+    v_load.wait()
+    count = 3 + (a + 1 < A).astype(jnp.int32) + (a > 0).astype(jnp.int32)
+    pl.semaphore_wait(barrier, count)
+
+    for i in range(3):
+        mate_copy(i, me).start()
+    for t in range(2):
+        for way in (ACROSS, UP, DOWN, SIDE):
+            go(t, me, way)
+
+    def tell(way, sg, k):
+        ahead = a + sg * k
+
+        def act():
+            pl.semaphore_signal(
+                token.at[way], inc=1, device_id={"seq": slot(a - sg, b, core)}, device_id_type=MESH
+            )
+
+        pl.when(jnp.logical_and(inside(ahead), inside(a - sg)))(act)
+
+    for way, sg in ((UP, 1), (DOWN, -1)):
+        tell(way, sg, 1)
+    acc[...] = jnp.zeros_like(acc)
+    den[...] = jnp.zeros_like(den)
+    top[...] = jnp.full_like(top, NEG)
+    tab = tab_ref[...]
+    fold = math.log2(math.e) / math.sqrt(HEAD)
+    q_cos, q_sin = cos_sin(pbuf[me][8 - frames :, :], tab)
+    q_cos, q_sin = q_cos * fold, q_sin * fold
+    for k in range(2, A):
+        for way, sg in ((UP, 1), (DOWN, -1)):
+            @pl.when(inside(a + sg * k))
+            def _(way=way):
+                pl.semaphore_wait(token.at[way], 1)
+
+            tell(way, sg, k)
+    for i in range(3):
+        mate_copy(i, mates[i]).wait_recv()
+    for k in range(1, A):
+        for sg in (1, -1):
+            x = a + sg * k
+            pl.when(inside(x))(lambda x=x: far_copy(x, a).start())
+
+    low = a < A // 2
+    mirror = jnp.where(low, a, A - 1 - a)
+
+    def plane_at(d):
+        near = -((d + 1) // 2) if d % 2 == 1 else d // 2
+        p = mirror + jnp.where(d <= 2 * mirror, near, d - mirror)
+        return jnp.where(low, p, A - 1 - p)
+
+    def along(d, t):
+        for sg in (1, -1):
+            x = a + sg * d
+
+            @pl.when(inside(x))
+            def _(x=x, sg=sg):
+                s = slot(x, b, core)
+                arrive(t, s)
+                go(t, s, DOWN if sg > 0 else UP)
+                go(t, s, ACROSS)
+                go(t, s, SIDE)
+
+    def crossed(p, t):
+        s = slot(p, 1 - b, core)
+        arrive(t, s)
+        go(t, s, SIDE)
+
+    def beside(p, t):
+        for y in range(2):
+            arrive(t, slot(p, y, 1 - core))
+
+    planes = [plane_at(d) for d in range(A)]
+
+    def event(j):
+        d, t = j // 2, j % 2
+        if d + 1 < A:
+            along(d + 1, t)
+        if d < A:
+            crossed(planes[d], t)
+
+    event(0)
+    event(1)
+    q_load.wait()
+    for x in range(A):
+        pl.when(x != a)(lambda x=x: far_copy(0, x).wait_recv())
+
+    everyone = pbuf[...].reshape(n * 8, HEAD)
+    angle = everyone * tab[32:33, :]
+    turns = jnp.round(angle * (1.0 / (2.0 * math.pi)))
+    angle = angle - turns * 6.28125
+    angle = angle - turns * (2.0 * math.pi - 6.28125)
+    sign = jnp.where(lane < HALF, -1.0, 1.0)
+    cosb[...] = jnp.cos(angle).reshape(n, 8, HEAD)
+    sinb[...] = (jnp.sin(angle) * sign).reshape(n, 8, HEAD)
+
+    for h in range(QH):
+        bias = pbuf[h // per, h % per : h % per + 1, :]
+        x = q_ref[:, h * HEAD : (h + 1) * HEAD].astype(jnp.float32) + bias
+        at = (h % RATIO) * rows
+        qs[h // RATIO, at : at + rows, :] = spin(x, q_cos, q_sin).astype(jnp.bfloat16)
+    share = n // KVH
+    k_bias = [sum(pbuf[g * share + i, 2:3, :] for i in range(share)) for g in range(KVH)]
+    v_bias = [sum(pbuf[g * share + i, 3:4, :] for i in range(share)) for g in range(KVH)]
+    within = lax.broadcasted_iota(jnp.int32, (FRAME_TOK, HEAD), 0).astype(jnp.float32)
+    temporal = lax.broadcasted_iota(jnp.int32, (FRAME_TOK, HEAD), 1) % HALF < PAIRS_T
+
+    def score(p):
+        for j in range(plane_size):
+            s = p * plane_size + j
+            order, cos_t, sin_t = pbuf[s], cosb[s], sinb[s]
+            cosine, sine = [], []
+            for f in range(frames):
+                r = 8 - frames + f
+                kpos = order[r : r + 1, :] * FRAME_TOK + within
+                at = j * rows + f * FRAME_TOK
+                hide[at : at + FRAME_TOK, :] = jnp.where(kpos <= qpos, 0.0, NEG)
+                cosine.append(jnp.where(temporal, cos_t[r : r + 1, :], tab[0:16, :]))
+                sine.append(jnp.where(temporal, sin_t[r : r + 1, :], tab[16:32, :]))
+            cosine, sine = jnp.concatenate(cosine, axis=0), jnp.concatenate(sine, axis=0)
+            for g in range(KVH):
+                x = kbuf[s, :, g * HEAD : (g + 1) * HEAD].astype(jnp.float32) + k_bias[g]
+                ksc[g, j * rows : (j + 1) * rows, :] = spin(x, cosine, sine).astype(jnp.bfloat16)
+        for g in range(KVH):
+            scores = lax.dot_general(
+                ksc[g], qs[g], (((1,), (1,)), ((), ())), preferred_element_type=jnp.float32
+            )
+            mask = hide[...]
+            scores = scores + jnp.concatenate([mask] * (scores.shape[1] // HEAD), axis=1)
+            old = top[g]
+            new = jnp.maximum(old, jnp.max(scores, axis=0, keepdims=True))
+            expo = jnp.exp2(scores - new)
+            factor = jnp.exp2(old - new)
+            top[g] = new
+            fac[g] = factor
+            den[g] = den[g] * factor + jnp.sum(expo, axis=0, keepdims=True)
+            prob[g] = expo.astype(jnp.bfloat16)
+
+    def mix(p):
+        for j in range(plane_size):
+            s = p * plane_size + j
+            for g in range(KVH):
+                y = vbuf[s, :, g * HEAD : (g + 1) * HEAD].astype(jnp.float32) + v_bias[g]
+                vsc[g, j * rows : (j + 1) * rows, :] = y.astype(jnp.bfloat16)
+        for g in range(KVH):
+            acc[g] = acc[g] * fac[g] + lax.dot_general(
+                vsc[g], prob[g], (((0,), (0,)), ((), ())), preferred_element_type=jnp.float32,
+            )
+
+    last = 2 * A
+    nxt = 2
+    event(nxt)
+    nxt += 1
+    for d in range(A):
+        p = planes[d]
+        while d == A - 1 and nxt < last:
+            event(nxt)
+            nxt += 1
+        beside(p, 0)
+        score(p)
+        if nxt < last - 1:
+            event(nxt)
+            nxt += 1
+        beside(p, 1)
+        mix(p)
+        if nxt < last - 1:
+            event(nxt)
+            nxt += 1
+
+    for g in range(KVH):
+        mixed = acc[g] * (1.0 / den[g])
+        flat = mixed.T.astype(jnp.bfloat16)
+        for r in range(RATIO):
+            h = g * RATIO + r
+            o_ref[:, h * HEAD : (h + 1) * HEAD] = flat[r * rows : (r + 1) * rows, :]
+
+    for i in range(3):
+        mate_copy(i, me).wait_send()
+    for k in range(1, A):
+        for sg in (1, -1):
+            x = a + sg * k
+            pl.when(inside(x))(lambda x=x: far_copy(x, a).wait_send())
+    for t in range(2):
+        for way in range(4):
+            when(ways[way][0], copy(t, me, way).wait_send)
+        for d in range(1, A):
+            for sg in (1, -1):
+                x = a + sg * d
+
+                @pl.when(inside(x))
+                def _(x=x, sg=sg, t=t):
+                    s = slot(x, b, core)
+                    way = DOWN if sg > 0 else UP
+                    when(ways[way][0], copy(t, s, way).wait_send)
+                    copy(t, s, ACROSS).wait_send()
+                    copy(t, s, SIDE).wait_send()
+
+        for p in planes:
+            copy(t, slot(p, 1 - b, core), SIDE).wait_send()
+
+
+def near_call(A, n, qper, *operands):
+    query, keys, query_bias, key_bias, frame_order = (operands[i] for i in (0, 1, 3, 4, 6))
+    rows = keys.shape[0]
+    wide = RATIO * rows
+    deep = 4 * rows
+    whole = pl.BlockSpec(memory_space=pltpu.VMEM)
+    far = pl.BlockSpec(memory_space=pltpu.HBM)
+    return pl.pallas_call(
+        functools.partial(near_kernel, A, n, qper),
+        out_shape=jax.ShapeDtypeStruct(query.shape, jnp.bfloat16),
+        in_specs=[far] * 8,
+        out_specs=whole,
+        scratch_shapes=[
+            pltpu.VMEM(query_bias.shape, jnp.bfloat16),
+            pltpu.VMEM(key_bias.shape, jnp.bfloat16),
+            pltpu.VMEM(key_bias.shape, jnp.bfloat16),
+            pltpu.SMEM(frame_order.shape, jnp.int32),
+            pltpu.VMEM((40, HEAD), jnp.float32),
+            pltpu.VMEM(query.shape, jnp.bfloat16),
+            pltpu.VMEM((n, rows, KVH * HEAD), jnp.bfloat16),
+            pltpu.VMEM((n, rows, KVH * HEAD), jnp.bfloat16),
+            pltpu.VMEM((n, 8, HEAD), jnp.float32),
+            pltpu.VMEM((n, 8, HEAD), jnp.float32),
+            pltpu.VMEM((n, 8, HEAD), jnp.float32),
+            pltpu.VMEM((KVH, wide, HEAD), jnp.bfloat16),
+            pltpu.VMEM((KVH, HEAD, wide), jnp.float32),
+            pltpu.VMEM((KVH, 1, wide), jnp.float32),
+            pltpu.VMEM((KVH, 1, wide), jnp.float32),
+            pltpu.VMEM((KVH, 1, wide), jnp.float32),
+            pltpu.VMEM((KVH, deep, HEAD), jnp.bfloat16),
+            pltpu.VMEM((KVH, deep, HEAD), jnp.bfloat16),
+            pltpu.VMEM((KVH, deep, wide), jnp.bfloat16),
+            pltpu.VMEM((deep, HEAD), jnp.float32),
+            pltpu.SemaphoreType.DMA((2, n)),
+            pltpu.SemaphoreType.DMA((2, 4, n)),
+            pltpu.SemaphoreType.DMA((3,)),
+            pltpu.SemaphoreType.DMA((3,)),
+            pltpu.SemaphoreType.DMA((A,)),
+            pltpu.SemaphoreType.DMA((A,)),
+            pltpu.SemaphoreType.DMA((8,)),
+            pltpu.SemaphoreType.REGULAR((2,)),
+        ],
+        compiler_params=pltpu.CompilerParams(vmem_limit_bytes=24 << 20, collective_id=0, has_side_effects=True),
+    )(*(
+        pltpu.with_memory_space_constraint(x, pltpu.HBM)
+        for x in operands + (jnp.asarray(tables()),)
+    ))
+
+
 def on_device(n, query, keys, values, query_bias, key_bias, value_projection_bias, frame_order):
     chips = n // 2
     B = 1
@@ -328,6 +694,8 @@
     A = chips // B
     rows = keys.shape[0]
     qper = query_bias.shape[0]
+    if B == 2 and qper >= HEAD:
+        return near_call(A, n, qper, query, keys, values, query_bias, key_bias, value_projection_bias, frame_order)
     wide = RATIO * rows
     keys_at_once = 4 * rows
     whole = pl.BlockSpec(memory_space=pltpu.VMEM)

time: 28.6 us -> 24.3 us (0.85)
  Pallas kernels: 27.7 us -> 23.3 us
    pallas_call x1, Pallas kernels: 27.7 us -> 23.3 us  [near_call(): pl.pallas_call(functools.partial(near_kernel, A, n, qper), out_shape=jax....]
where the time goes in v1:
time: 24.3 us; the launch traced here: 24.1 us
  Pallas kernels  23.3 us (96%)
  local copies, waits for them, and re-layouts  0.8 us (3%)
    pallas_call x1, Pallas kernels, near_call(): pl.pallas_call(functools.partial(near_kernel, A, n, qper), out_shape=jax....  23.3 us
    unnamed x1, local copies, waits for them, and re-layouts  0.8 us

profile of v1, /device:TPU:1, one launch (start us, length us, event | category | flops | bytes accessed | tf_op | source)
XLA Modules:
  0.0 24.1 jit_solution(6432545191724518844)
XLA Ops:
  0.0 23.3 %shard_map.82 = bf16[64,4096]{1,0:T(8,128)(2,1)S(1)} custom-call(bf16[64,4096]{1,0:T(8,128)(2,1)} %q_hbm.1, bf16[64,512]{1,0:T(8,128)(2,1)} %k_hbm.1, bf16[64,512]{1,0:T(8,128)(2,1)} %v_hbm.1, bf16[256]{0:T(256)(128)(2,1)} %qb_hbm.1, bf16[32]{0:T(256)(128)(2,1)} %kb_hbm.1, bf16[32]{0:T(256)(128)(2,1)} %vb_hbm.1, s32[4]{0:T(128)} %order_hbm.1, ...), custom_call_target="tpu_custom_call" | custom-call | tf_op jit(solution)/shard_map/pallas_call | solution.py:647
  23.3 0.8 %copy.10 = bf16[64,4096]{1,0:T(8,128)(2,1)} copy(bf16[64,4096]{1,0:T(8,128)(2,1)S(1)} %shard_map.82) | data formatting | bytes 1048576
